TPU v7x, 256 devices: a whole 4x4x8 slice. The times are simulated.
256 devices in a mesh: seq: 64 (over y, z, core), tensor: 4 (over x).
Axes of the slice: x: 4, y: 4, z: 8, core: 2. Of those that a mesh axis runs over, the one named last changes fastest.
Arguments:
- tokens: bfloat16 [32768, 3840], P('seq', 'tensor'), may hold values from -6 to 6
- w_query: bfloat16 [3840, 2048], P(None, 'tensor'), may hold values from -0.09375 to 0.09375
- w_key: bfloat16 [3840, 1024], P(None, 'tensor'), may hold values from -0.09375 to 0.09375
- w_value: bfloat16 [3840, 1024], P(None, 'tensor'), may hold values from -0.09375 to 0.09375
- query_gain: float32 [256], replicated, may hold values from 0.1 to 1.9
- key_gain: float32 [256], replicated, may hold values from 0.1 to 1.9
- adapter_down: bfloat16 [64, 64, 3840], P('seq', None, 'tensor'), may hold values from -0.09375 to 0.09375
- adapter_up: bfloat16 [64, 64, 2048], P('seq', None, 'tensor'), may hold values from -0.75 to 0.75
- adapter_ids: int32 [32768, 1], P('seq'), may hold values from 0 to 63; in each aligned block of 512 rows (0 to 511, 512 to 1023, ...) at most 16 rows name the same one
- doc_ids: int32 [32768], P('seq'), may hold values from 0 to 63, never falling along the last dimension, each value on 1 to 4096 neighbouring positions
- cotangent: bfloat16 [32768, 2048], P('seq', 'tensor'), may hold values from -6 to 6
Outputs:
- attended: bfloat16 [32768, 2048], P('seq', 'tensor')
- grad_up: float32 [64, 64, 2048], P('seq', None, 'tensor')
Inputs may be any that keep to these rules, and one draw needn't show every extreme that they name: `adapter_ids`: within the 512 tokens of one device no adapter is named by more than 16 tokens; in every draw some adapter is named by exactly 16 tokens of some device. `doc_ids`: document numbers never fall along the slab; each document has 1 to 4096 tokens and one has exactly 4096.
All inputs are finite; a program needn't handle non-finite values.
Results may differ from a plain program's by a relative error of at most 0.0088.
Values may be sent and summed in bfloat16 or wider, within the bound.
A program may use at most 128 MiB of HBM per device.

v0:
```python
import math
import jax
import jax.numpy as jnp
from jax import lax
from jax.sharding import PartitionSpec as P

HD = 256
R = 64
WINDOW = 1024
ADAPTERS = 64
CAP = 16


def passed_along(value, axis, steps):
    count = lax.axis_size(axis)
    first, last = (max(0, -steps), min(count, count - steps))
    return lax.ppermute(value, axis, [(source, source + steps) for source in range(first, last)])


def normalize(pre_field, gain_vec):
    mean_sq = jnp.mean(pre_field * pre_field, axis=-1, keepdims=True)
    return pre_field * lax.rsqrt(mean_sq + 1e-06) * gain_vec


def rotate(pre_field, positions):
    half_dim = pre_field.shape[-1] // 2
    frequency = jnp.exp(
        jnp.arange(half_dim, dtype=jnp.float32) * (-2.0 * math.log(10000.0) / pre_field.shape[-1])
    )
    angles = positions.astype(jnp.float32)[:, None] * frequency[None, :]
    cosine = jnp.cos(angles)[:, None, :]
    sine_part = jnp.sin(angles)[:, None, :]
    lower_half = pre_field[..., :half_dim]
    second = pre_field[..., half_dim:]
    return jnp.concatenate(
        [lower_half * cosine - second * sine_part, second * cosine + lower_half * sine_part],
        axis=-1,
    )


def shape_query(pre_field, gain_vec, positions):
    return rotate(normalize(pre_field, gain_vec), positions)


def attend(queries, key_rows, values, upstream, allowed):
    score_scale = 1.0 / math.sqrt(queries.shape[-1])
    scores = (
        jnp.einsum("tngd,knd->ngtk", queries, key_rows, preferred_element_type=jnp.float32)
        * score_scale
    )
    weights = jnp.where(allowed[None, None], jnp.exp(scores), 0.0)
    probs = weights / jnp.sum(weights, axis=-1, keepdims=True)
    probs_low = probs.astype(jnp.bfloat16)
    attended = jnp.einsum("ngtk,knd->tngd", probs_low, values, preferred_element_type=jnp.float32)
    dprobs = jnp.einsum("tngd,knd->ngtk", upstream, values, preferred_element_type=jnp.float32)
    delta = jnp.sum(probs * dprobs, axis=-1, keepdims=True)
    dscores = (probs * (dprobs - delta) * score_scale).astype(jnp.bfloat16)
    dqueries = jnp.einsum("ngtk,knd->tngd", dscores, key_rows, preferred_element_type=jnp.float32)
    return (attended.astype(jnp.bfloat16), dqueries)


def local(
    tokens,
    w_query,
    w_key,
    w_value,
    query_gain,
    key_gain,
    adapter_down,
    adapter_up,
    adapter_ids,
    doc_ids,
    cotangent,
):
    tok_count = tokens.shape[0]
    feat_width = tokens.shape[1]
    q_width = w_query.shape[1]
    kv_width = w_key.shape[1]
    local_heads = q_width // HD
    kv_heads = kv_width // HD
    head_group = local_heads // kv_heads
    positions = lax.axis_index("seq") * tok_count + jnp.arange(tok_count, dtype=jnp.int32)
    shard_cols = lax.all_gather(tokens, "tensor", axis=1, tiled=True)
    query_lin = jnp.dot(shard_cols, w_query, preferred_element_type=jnp.float32)
    key_lin = jnp.dot(shard_cols, w_key, preferred_element_type=jnp.float32)
    value_lin = jnp.dot(shard_cols, w_value, preferred_element_type=jnp.float32)
    token_adapter = adapter_ids[:, 0]
    chosen = token_adapter[:, None] == jnp.arange(ADAPTERS, dtype=jnp.int32)[None, :]
    before = jnp.cumsum(chosen.astype(jnp.int32), axis=0) - 1
    slot_rank = jnp.sum(jnp.where(chosen, before, 0), axis=1)
    slot_index = token_adapter * CAP + slot_rank
    dispatch = (slot_index[None, :] == jnp.arange(ADAPTERS * CAP, dtype=jnp.int32)[:, None]).astype(
        jnp.bfloat16
    )
    outgoing = jnp.dot(dispatch, tokens, preferred_element_type=jnp.float32).astype(jnp.bfloat16)
    all_down, all_up = (
        lax.all_gather(adapter_down, "seq", axis=0, tiled=True),
        lax.all_gather(adapter_up, "seq", axis=0, tiled=True),
    )
    slot_rows = outgoing.reshape(ADAPTERS, CAP, feat_width)
    partial_low = jnp.einsum(
        "acd,ard->acr", slot_rows, all_down, preferred_element_type=jnp.float32
    )
    slot_low = lax.psum(partial_low, "tensor").astype(jnp.bfloat16)
    slot_lift = jnp.einsum(
        "acr,are->ace", slot_low, all_up, preferred_element_type=jnp.float32
    ).astype(jnp.bfloat16)
    lifted = jnp.einsum(
        "st,se->te",
        dispatch,
        slot_lift.reshape(ADAPTERS * CAP, q_width),
        preferred_element_type=jnp.float32,
    ).astype(jnp.bfloat16)
    lowrank = jnp.einsum(
        "st,sr->tr",
        dispatch,
        slot_low.reshape(ADAPTERS * CAP, R),
        preferred_element_type=jnp.float32,
    ).astype(jnp.bfloat16)
    query_pre = (query_lin + lifted.astype(jnp.float32)).reshape(tok_count, local_heads, HD)
    queries, query_back = jax.vjp(
        lambda pre_query: shape_query(pre_query, query_gain, positions), query_pre
    )
    queries = queries.astype(jnp.bfloat16).reshape(tok_count, kv_heads, head_group, HD)
    key_rows = shape_query(key_lin.reshape(tok_count, kv_heads, HD), key_gain, positions).astype(
        jnp.bfloat16
    )
    values = value_lin.astype(jnp.bfloat16).reshape(tok_count, kv_heads, HD)
    rim_count = WINDOW // tok_count
    key_list = []
    value_list = []
    doc_list = []
    place_list = []
    for distance in range(rim_count, 0, -1):
        far_keys, far_values, far_docs = passed_along((key_rows, values, doc_ids), "seq", distance)
        key_list.append(far_keys)
        value_list.append(far_values)
        doc_list.append(far_docs)
        place_list.append(positions - distance * tok_count)
    key_list.append(key_rows)
    value_list.append(values)
    doc_list.append(doc_ids)
    place_list.append(positions)
    window_keys = jnp.concatenate(key_list, axis=0)
    window_values = jnp.concatenate(value_list, axis=0)
    key_docs = jnp.concatenate(doc_list, axis=0)
    key_pos = jnp.concatenate(place_list, axis=0)
    key_gap = positions[:, None] - key_pos[None, :]
    allowed = (
        (doc_ids[:, None] == key_docs[None, :])
        & (key_gap >= 0)
        & (key_gap < WINDOW)
        & (key_pos[None, :] >= 0)
    )
    upstream = cotangent.reshape(tok_count, kv_heads, head_group, HD)
    block_out, dqueries = attend(queries, window_keys, window_values, upstream, allowed)
    attended = block_out.reshape(tok_count, q_width)
    (dquery_pre,) = query_back(dqueries.reshape(tok_count, local_heads, HD))
    dquery_pre = dquery_pre.reshape(tok_count, q_width).astype(jnp.bfloat16)
    out_low = jnp.dot(dispatch, lowrank, preferred_element_type=jnp.float32).astype(jnp.bfloat16)
    out_grad = jnp.dot(dispatch, dquery_pre, preferred_element_type=jnp.float32).astype(
        jnp.bfloat16
    )
    slot_low_rows = out_low.reshape(ADAPTERS, CAP, R)
    slot_grad_rows = out_grad.reshape(ADAPTERS, CAP, q_width)
    grad_up = lax.psum_scatter(
        jnp.einsum(
            "acr,ace->are", slot_low_rows, slot_grad_rows, preferred_element_type=jnp.float32
        ),
        "seq",
        scatter_dimension=0,
        tiled=True,
    )
    return (attended, grad_up)


def solution(mesh):
    in_specs = (
        P("seq", "tensor"),
        P(None, "tensor"),
        P(None, "tensor"),
        P(None, "tensor"),
        P(),
        P(),
        P("seq", None, "tensor"),
        P("seq", None, "tensor"),
        P("seq", None),
        P("seq"),
        P("seq", "tensor"),
    )
    out_specs = (P("seq", "tensor"), P("seq", None, "tensor"))
    return jax.shard_map(local, mesh=mesh, in_specs=in_specs, out_specs=out_specs, check_vma=False)
```

profile of v0, /device:TPU:2, one launch (start us, length us, event | category | flops | bytes accessed | tf_op | source)
XLA Modules:
  0.0 409.1 jit_solution(11032409171625994337)
XLA Ops:
  9.4 1.7 collective-permute-start.3
  11.2 4.0 collective-permute-start.2
  15.9 1.2 reduce-window.6
  17.4 0.8 fusion.59
  18.9 1.0 multiply_cosine_fusion
  19.9 3.7 fusion.24
  23.7 4.0 copy.40
  27.7 2.5 fusion.16
  30.2 30.4 %all-gather.4.cloned.1.call-done = bf16[512,3840]{0,1:T(8,128)(2,1)} async-done(((bf16[512,960]{0,1:T(8,128)(2,1)}), bf16[512,3840]{0,1:T(8,128)(2,1)}) %all-gather.4.cloned.1.call-update) | async-done | bytes 3932176 | tf_op jit(solution)/shard_map/all_gather | solution.py:83
  60.7 3.5 multiply_reduce_fusion.2
  64.3 1.2 fusion.55
  66.2 2.3 collective-permute-start.5
  68.5 3.8 collective-permute-start.4
  72.3 1.9 fusion.34
  74.2 4.0 collective-permute-start.1
  78.2 2.8 collective-permute-start
  81.0 66.8 %all-gather.6.cloned.1.call-done = bf16[64,64,960]{2,1,0:T(8,128)(2,1)} async-done(((bf16[1,64,960]{2,1,0:T(8,128)(2,1)}), bf16[64,64,960]{2,1,0:T(8,128)(2,1)}) %all-gather.6.cloned.1.call-update) | async-done | bytes 7864336 | tf_op jit(solution)/shard_map/all_gather | solution.py:97
  147.8 6.3 %fusion.73 = f32[64,16,64]{2,1,0:T(8,128)S(1)} fusion(bf16[64,16,960]{2,1,0:T(8,128)(2,1)} %bitcast.128, bf16[64,64,960]{2,1,0:T(8,128)(2,1)} %all-gather.6.cloned.1.call-done), kind=kOutput, calls=%fused_computation.106 | convolution fusion | flops 125829120 | bytes 10092544 | tf_op jit(solution)/shard_map/acd,ard->acr/dot_general | solution.py:101
  154.1 20.2 %all-reduce.3 = bf16[64,16,64]{2,1,0:T(8,128)(2,1)S(1)} all-reduce(f32[64,16,64]{2,1,0:T(8,128)S(1)} %fusion.73), channel_id=1, replica_groups=mesh['seq'=64,'tensor'=4] {'tensor'}, use_global_device_ids=true, to_apply=%region_4.5 | all-reduce | flops 65536 | bytes 393216 | tf_op jit(solution)/shard_map/psum | solution.py:104
  174.4 52.3 %all-gather.8.cloned.1.call-done = bf16[64,64,512]{2,1,0:T(8,128)(2,1)} async-done(((bf16[1,64,512]{2,1,0:T(8,128)(2,1)}), bf16[64,64,512]{2,1,0:T(8,128)(2,1)}) %all-gather.8.cloned.1.call-update) | async-done | bytes 4194320 | tf_op jit(solution)/shard_map/all_gather | solution.py:98
  226.7 3.0 convolution_convert_fusion
  229.7 0.8 fusion.30
  230.5 0.8 copy-done.8
  231.2 2.3 multiply_reduce_fusion.1
  233.9 0.9 fusion.35
  235.3 3.1 fusion.5
  238.5 4.4 %fusion = (f32[2,512]{1,0:T(2,128)S(1)}, f32[1536,512,2]{1,0,2:T(8,128)S(1)}) fusion(f32[2,512]{1,0:T(2,128)S(1)} %get-tuple-element.20, f32[1536,512,2]{1,0,2:T(8,128)S(1)} %get-tuple-element.21, pred[512,1536]{0,1:T(8,128)(4,1)S(1)} %copy-done.2, bf16[64,2,8,256]{3,2,1,0:T(8,128)(2,1)S(1)} %bitcast.139, bf16[512,1,256]{2,0,1:T(8,128)(2,1)} %fusion.34, ...), kind=kOutput, calls=%fused_computation.3 | convolution fusion | flops 815528960 | bytes 14688256 | tf_op jit(solution)/shard_map/tngd,knd->ngtk/dot_general | solution.py:55
  242.9 3.8 fusion.26
  248.4 4.5 %fusion.74 = f32[64,64,512]{2,1,0:T(8,128)} fusion(bf16[64,16,64]{2,1,0:T(8,128)(2,1)S(1)} %bitcast.130, bf16[64,16,512]{2,1,0:T(8,128)(2,1)S(1)} %bitcast.129), kind=kOutput, calls=%fused_computation.107 | convolution fusion | flops 67108864 | bytes 9568256 | tf_op jit(solution)/shard_map/acr,ace->are/dot_general | solution.py:167
  253.0 5.2 %fusion.31 = bf16[256,2,512]{2,0,1:T(8,128)(2,1)S(1)} fusion(f32[2,512]{1,0:T(2,128)S(1)} %get-tuple-element.20, f32[1536,512,2]{1,0,2:T(8,128)} %copy-done.11, pred[512,1536]{0,1:T(8,128)(4,1)S(1)} %copy-done.2, bf16[512,1,256]{2,0,1:T(8,128)(2,1)} %fusion.34, bf16[512,1,256]{2,0,1:T(8,128)(2,1)} %collective-permute-done.1, ...), kind=kOutput, calls=%fused_computation.35 | convolution fusion | flops 814219264 | bytes 8392704 | tf_op jit(solution)/shard_map/ngtk,knd->tngd/dot_general | solution.py:54
  258.2 1.0 copy.52
  259.2 143.4 %reduce-scatter.2.cloned.1.call-done = f32[1,64,512]{2,1,0:T(8,128)} async-done(((f32[64,64,512]{2,1,0:T(8,128)}), f32[1,64,512]{2,1,0:T(8,128)}) %reduce-scatter.2.cloned.1.call-update) | async-done | bytes 131088 | tf_op jit(solution)/shard_map/reduce_scatter | solution.py:166
  (63 shorter events, 7.4 us)
Async XLA Ops:
  7.2 53.5 %copy-start = (bf16[3840,256]{1,0:T(8,128)(2,1)S(1)}, bf16[3840,256]{1,0:T(8,128)(2,1)}, u32[]{:S(2)}) copy-start(bf16[3840,256]{1,0:T(8,128)(2,1)} %param.13) | copy-start | bytes 5898244
  7.2 53.5 %all-gather.4.cloned.1.call-start = ((), (), s32[]{:S(2)}) async-start(), calls=%async_computation.1 | async-start | bytes 4915200 | tf_op jit(solution)/shard_map/all_gather | solution.py:83
  7.9 139.9 %all-gather.6.cloned.1.call-start = ((), (), s32[]{:S(2)}) async-start(), calls=%async_computation.2 | async-start | bytes 8519680 | tf_op jit(solution)/shard_map/all_gather | solution.py:97
  8.7 218.0 %all-gather.8.cloned.1.call-start = ((), (), s32[]{:S(2)}) async-start(), calls=%async_computation.3 | async-start | bytes 4259840 | tf_op jit(solution)/shard_map/all_gather | solution.py:98
  9.4 393.2 %reduce-scatter.2.cloned.1.call-start = ((), (), s32[]{:S(2)}) async-start(), calls=%async_computation.4 | async-start | bytes 8519680 | tf_op jit(solution)/shard_map/reduce_scatter | solution.py:166
  9.4 18.2 %collective-permute-start.3 = (s32[512]{0:T(512)}, s32[512]{0:T(512)S(1)}, u32[]{:S(2)}, u32[]{:S(2)}) collective-permute-start(s32[512]{0:T(512)} %param.20), channel_id=1, source_target_pairs={{0,4},{4,8},{8,12},{12,16},{16,20},{20,24},{24,28},{28,32},{32,36}... | collective-permute-start | bytes 6152 | tf_op jit(solution)/shard_map/ppermute | solution.py:17
  11.2 16.5 %collective-permute-start.2 = (s32[512]{0:T(512)}, s32[512]{0:T(512)S(1)}, u32[]{:S(2)}, u32[]{:S(2)}) collective-permute-start(s32[512]{0:T(512)} %param.20), channel_id=1, source_target_pairs={{0,8},{4,12},{8,16},{12,20},{16,24},{20,28},{24,32},{28,36},{32,40... | collective-permute-start | bytes 6152 | tf_op jit(solution)/shard_map/ppermute | solution.py:17
  23.7 4.0 copy-start.4
  30.2 34.0 %copy-start.5 = (f32[256]{0:T(256)S(1)}, f32[256]{0:T(256)}, u32[]{:S(2)}) copy-start(f32[256]{0:T(256)} %param.16) | copy-start | bytes 3076
  60.7 11.6 %copy-start.7 = (bf16[512,3840]{0,1:T(8,128)(2,1)S(1)}, bf16[512,3840]{0,1:T(8,128)(2,1)}, u32[]{:S(2)}) copy-start(bf16[512,3840]{0,1:T(8,128)(2,1)} %all-gather.4.cloned.1.call-done) | copy-start | bytes 11796484
  60.7 11.6 %copy-start.9 = (bf16[3840,256]{1,0:T(8,128)(2,1)S(1)}, bf16[3840,256]{1,0:T(8,128)(2,1)}, u32[]{:S(2)}) copy-start(bf16[3840,256]{1,0:T(8,128)(2,1)} %param.14) | copy-start | bytes 5898244
  66.2 169.1 %collective-permute-start.5 = (bf16[512,1,256]{0,2,1:T(8,128)(2,1)}, bf16[512,1,256]{0,2,1:T(8,128)(2,1)}, u32[]{:S(2)}, u32[]{:S(2)}) collective-permute-start(bf16[512,1,256]{0,2,1:T(8,128)(2,1)} %pad_maximum_fusion), channel_id=1, source_target_pairs={{0,4},{4,8},{8,12},{12,16},{16,20},{20,24},{24,28},{28,32},{32,36}... | collective-permute-start | bytes 786440 | tf_op jit(solution)/shard_map/ppermute | solution.py:17
  68.5 166.8 %collective-permute-start.4 = (bf16[512,1,256]{0,2,1:T(8,128)(2,1)}, bf16[512,1,256]{0,2,1:T(8,128)(2,1)}, u32[]{:S(2)}, u32[]{:S(2)}) collective-permute-start(bf16[512,1,256]{0,2,1:T(8,128)(2,1)} %pad_maximum_fusion), channel_id=1, source_target_pairs={{0,8},{4,12},{8,16},{12,20},{16,24},{20,28},{24,32},{28,36},{32,40... | collective-permute-start | bytes 786440 | tf_op jit(solution)/shard_map/ppermute | solution.py:17
  74.2 164.2 %collective-permute-start.1 = (bf16[512,1,256]{2,0,1:T(8,128)(2,1)}, bf16[512,1,256]{2,0,1:T(8,128)(2,1)}, u32[]{:S(2)}, u32[]{:S(2)}) collective-permute-start(bf16[512,1,256]{2,0,1:T(8,128)(2,1)} %fusion.34), channel_id=1, source_target_pairs={{0,4},{4,8},{8,12},{12,16},{16,20},{20,24},{24,28},{28,32},{32,36}... | collective-permute-start | bytes 786440 | tf_op jit(solution)/shard_map/ppermute | solution.py:17
  78.2 160.2 %collective-permute-start = (bf16[512,1,256]{2,0,1:T(8,128)(2,1)}, bf16[512,1,256]{2,0,1:T(8,128)(2,1)}, u32[]{:S(2)}, u32[]{:S(2)}) collective-permute-start(bf16[512,1,256]{2,0,1:T(8,128)(2,1)} %fusion.34), channel_id=1, source_target_pairs={{0,8},{4,12},{8,16},{12,20},{16,24},{20,28},{24,32},{28,36},{32,40... | collective-permute-start | bytes 786440 | tf_op jit(solution)/shard_map/ppermute | solution.py:17
  226.7 3.8 copy-start.6
  226.7 4.6 %copy-start.8 = (bf16[512,3840]{0,1:T(8,128)(2,1)S(1)}, bf16[512,3840]{0,1:T(8,128)(2,1)}, u32[]{:S(2)}) copy-start(bf16[512,3840]{0,1:T(8,128)(2,1)} %all-gather.4.cloned.1.call-done) | copy-start | bytes 11796484
  233.5 1.4 copy-start.3
  233.8 1.5 copy-start.2
  235.3 3.1 copy-start.10
  238.4 4.5 %copy-start.11 = (f32[1536,512,2]{1,0,2:T(8,128)}, f32[1536,512,2]{1,0,2:T(8,128)S(1)}, u32[]{:S(2)}) copy-start(f32[1536,512,2]{1,0,2:T(8,128)S(1)} %get-tuple-element.21) | copy-start | bytes 18874372
  253.0 149.6 %copy-start.1 = (bf16[3840,256]{1,0:T(8,128)(2,1)S(1)}, bf16[3840,256]{1,0:T(8,128)(2,1)}, u32[]{:S(2)}) copy-start(bf16[3840,256]{1,0:T(8,128)(2,1)} %param.13) | copy-start | bytes 5898244
Sparse Core Ops, SparseCore 0:
  9.8 50.8 all-gather.3
  63.4 84.3 all-gather.5
  150.6 76.0 all-gather.7
  253.1 149.4 reduce-scatter.1
where the time goes:
time: 410 us; the launch traced here: 409 us
  waiting for transfers between devices  295 us (72%)
  matrix products  44.1 us (11%)
  blocking collectives  20.2 us (5%)
  starting transfers between devices  18.7 us (5%)
  between operations  14.1 us (3%)
  other arithmetic  10.1 us (2%)
  local copies, waits for them, and re-layouts  6.79 us (2%)
    reduce_scatter x1, waiting for transfers between devices, local(): lax.psum_scatter(jnp.einsum('acr,ace->are', slot_low_rows, slot_grad_rows...  143 us
    all_gather x1, waiting for transfers between devices, local(): lax.all_gather(adapter_down, 'seq', axis=0, tiled=True)  66.8 us
    all_gather x1, waiting for transfers between devices, local(): lax.all_gather(adapter_up, 'seq', axis=0, tiled=True)  52.3 us
    all_gather x1, waiting for transfers between devices, local(): shard_cols = lax.all_gather(tokens, 'tensor', axis=1, tiled=True)  30.4 us
    psum x1, blocking collectives, local(): slot_low = lax.psum(partial_low, 'tensor').astype(jnp.bfloat16)  20.2 us
    ppermute x6, starting transfers between devices, passed_along(): lax.ppermute(value, axis, [(source, source + steps) for source in range(f...  18.6 us
  transfers between devices with their start and end apart: 10, of which 4 were waited for; matrix products, arithmetic and copies ran while one was open for 11% of the time, Pallas kernels for 0%

commit v1 on v0

--- a/solution.py
+++ b/solution.py
@@ -9,6 +9,28 @@
 WINDOW = 1024
 ADAPTERS = 64
 CAP = 16
+
+
+def joined_along(tiles, dim):
+    shape = list(tiles.shape[1:])
+    shape[dim] *= tiles.shape[0]
+    return jnp.moveaxis(tiles, 0, dim).reshape(shape)
+
+
+def gather_around(x, axis, dim):
+    size = lax.axis_size(axis)
+    pairs = [(i, (i + 1) % size) for i in range(size)]
+    back = [(b, a) for a, b in pairs]
+    lower, upper = ([], [])
+    for step in range(size - 1):
+        if step % 2 == 0:
+            lower.append(lax.ppermute(lower[-1] if lower else x, axis, pairs))
+        else:
+            upper.append(lax.ppermute(upper[-1] if upper else x, axis, back))
+    pieces = jnp.stack([*lower[::-1], x, *upper])
+    shift = lax.axis_index(axis) - len(lower)
+    pieces = pieces[(jnp.arange(size) - shift) % size]
+    return joined_along(pieces, dim)
 
 
 def passed_along(value, axis, steps):
@@ -80,7 +102,7 @@
     kv_heads = kv_width // HD
     head_group = local_heads // kv_heads
     positions = lax.axis_index("seq") * tok_count + jnp.arange(tok_count, dtype=jnp.int32)
-    shard_cols = lax.all_gather(tokens, "tensor", axis=1, tiled=True)
+    shard_cols = gather_around(tokens, "tensor", 1)
     query_lin = jnp.dot(shard_cols, w_query, preferred_element_type=jnp.float32)
     key_lin = jnp.dot(shard_cols, w_key, preferred_element_type=jnp.float32)
     value_lin = jnp.dot(shard_cols, w_value, preferred_element_type=jnp.float32)

time: 410 us -> 362 us (0.88)
  waiting for transfers between devices: 295 us -> 234 us
  local copies, waits for them, and re-layouts: 6.79 us -> 11.6 us
  starting transfers between devices: 18.7 us -> 23.3 us
    all_gather x1, waiting for transfers between devices: 66.8 us -> 4.1 us  [local(): lax.all_gather(adapter_down, 'seq', axis=0, tiled=True)]
    ppermute x0 -> x3, waiting for transfers between devices: none -> 33.8 us  [the longest x2 33.8 us: gather_around(): lower.append(lax.ppermute(lower[-1] if lower else x, axis, pairs))]
    all_gather x1 -> x0, waiting for transfers between devices: 30.4 us -> none  [local(): shard_cols = lax.all_gather(tokens, 'tensor', axis=1, tiled=True)]
    gather x0 -> x1, local copies, waits for them, and re-layouts: none -> 4.9 us  [gather_around(): pieces = pieces[(jnp.arange(size) - shift) % size]]
  transfers between devices with their start and end apart: 10 -> 12, of which waited for: 4 -> 5; matrix products, arithmetic and copies ran while one was open for 11% -> 15% of each run, Pallas kernels for 0% -> 0%
where the time goes in v1:
time: 362 us; the launch traced here: 361 us
  waiting for transfers between devices  234 us (65%)
  matrix products  44.1 us (12%)
  starting transfers between devices  23.3 us (6%)
  blocking collectives  20.7 us (6%)
  between operations  14.1 us (4%)
  other arithmetic  13.7 us (4%)
  local copies, waits for them, and re-layouts  11.6 us (3%)
    reduce_scatter x1, waiting for transfers between devices, local(): lax.psum_scatter(jnp.einsum('acr,ace->are', slot_low_rows, slot_grad_rows...  143 us
    all_gather x1, waiting for transfers between devices, local(): lax.all_gather(adapter_up, 'seq', axis=0, tiled=True)  51 us
    ppermute x2, waiting for transfers between devices, gather_around(): lower.append(lax.ppermute(lower[-1] if lower else x, axis, pairs))  33.8 us
    psum x1, blocking collectives, local(): slot_low = lax.psum(partial_low, 'tensor').astype(jnp.bfloat16)  20.7 us
    ppermute x6, starting transfers between devices, passed_along(): lax.ppermute(value, axis, [(source, source + steps) for source in range(f...  20 us
  transfers between devices with their start and end apart: 12, of which 5 were waited for; matrix products, arithmetic and copies ran while one was open for 15% of the time, Pallas kernels for 0%

profile of v1, /device:TPU:2, one launch (start us, length us, event | category | flops | bytes accessed | tf_op | source)
XLA Modules:
  0.0 361.2 jit_solution(6627960136760291712)
XLA Ops:
  8.7 1.7 collective-permute-start.6
  10.5 4.0 %collective-permute-start.5 = (s32[512]{0:T(512)}, s32[512]{0:T(512)S(1)}, u32[]{:S(2)}, u32[]{:S(2)}) collective-permute-start(s32[512]{0:T(512)} %param.20), channel_id=1, source_target_pairs={{0,8},{4,12},{8,16},{12,20},{16,24},{20,28},{24,32},{28,36},{32,40... | collective-permute-start | bytes 6152 | tf_op jit(solution)/shard_map/ppermute | solution.py:39
  15.1 1.5 collective-permute-start
  17.3 1.2 reduce-window.6
  20.3 3.8 %fusion.24 = bf16[1024,960]{0,1:T(8,128)(2,1)} fusion(bf16[512,960]{0,1:T(8,128)(2,1)} %param.11, s32[512]{0:T(512)S(1)} %multiply_add_fusion.3), kind=kOutput, calls=%fused_computation.29 | convolution fusion | flops 1008140288 | bytes 2951168 | tf_op jit(solution)/shard_map/dot_general | solution.py:117
  24.1 16.0 %collective-permute-done = bf16[512,960]{0,1:T(8,128)(2,1)} collective-permute-done((bf16[512,960]{0,1:T(8,128)(2,1)}, bf16[512,960]{0,1:T(8,128)(2,1)}, u32[]{:S(2)}, u32[]{:S(2)}) %collective-permute-start) | collective-permute-done | bytes 983072 | tf_op jit(solution)/shard_map/ppermute | solution.py:27
  40.0 1.0 collective-permute-start.1
  42.0 3.9 %copy.40 = bf16[1024,960]{1,0:T(8,128)(2,1)} copy(bf16[1024,960]{0,1:T(8,128)(2,1)} %fusion.24) | data formatting | bytes 3932160 | tf_op jit(solution)/shard_map/convert_element_type | solution.py:117
  46.0 2.5 fusion.16
  48.5 17.8 %collective-permute-done.1 = bf16[512,960]{0,1:T(8,128)(2,1)} collective-permute-done((bf16[512,960]{0,1:T(8,128)(2,1)}, bf16[512,960]{0,1:T(8,128)(2,1)}, u32[]{:S(2)}, u32[]{:S(2)}) %collective-permute-start.1) | collective-permute-done | bytes 983072 | tf_op jit(solution)/shard_map/ppermute | solution.py:27
  66.3 3.5 pad_maximum_fusion
  69.9 4.9 %gather_fusion = bf16[4,512,960]{1,2,0:T(8,128)(2,1)} fusion(bf16[4,512,960]{1,2,0:T(8,128)(2,1)} %pad_maximum_fusion, s32[1024]{0:T(1024)S(1)} %pad_clamp_fusion), kind=kCustom, calls=%fused_computation | custom fusion | bytes 7864336 | tf_op jit(solution)/shard_map/gather | solution.py:32
  74.8 3.5 multiply_reduce_fusion.2
  78.5 1.2 fusion.55
  80.4 2.6 collective-permute-start.8
  83.0 3.5 collective-permute-start.7
  86.5 1.9 fusion.34
  88.4 2.6 collective-permute-start.4
  91.0 5.6 %collective-permute-start.3 = (bf16[512,1,256]{2,0,1:T(8,128)(2,1)}, bf16[512,1,256]{2,0,1:T(8,128)(2,1)}, u32[]{:S(2)}, u32[]{:S(2)}) collective-permute-start(bf16[512,1,256]{2,0,1:T(8,128)(2,1)} %fusion.34), channel_id=1, source_target_pairs={{0,8},{4,12},{8,16},{12,20},{16,24},{20,28},{24,32},{28,36},{32,40... | collective-permute-start | bytes 786440 | tf_op jit(solution)/shard_map/ppermute | solution.py:39
  96.6 4.1 %all-gather.3.cloned.1.call-done = bf16[64,64,960]{2,1,0:T(8,128)(2,1)} async-done(((bf16[1,64,960]{2,1,0:T(8,128)(2,1)}), bf16[64,64,960]{2,1,0:T(8,128)(2,1)}) %all-gather.3.cloned.1.call-update) | async-done | bytes 7864336 | tf_op jit(solution)/shard_map/all_gather | solution.py:119
  100.7 6.3 %fusion.75 = f32[64,16,64]{2,1,0:T(8,128)S(1)} fusion(bf16[64,16,960]{2,1,0:T(8,128)(2,1)} %bitcast.137, bf16[64,64,960]{2,1,0:T(8,128)(2,1)} %all-gather.3.cloned.1.call-done), kind=kOutput, calls=%fused_computation.115 | convolution fusion | flops 125829120 | bytes 10092544 | tf_op jit(solution)/shard_map/acd,ard->acr/dot_general | solution.py:123
  107.0 20.7 %all-reduce.3 = bf16[64,16,64]{2,1,0:T(8,128)(2,1)S(1)} all-reduce(f32[64,16,64]{2,1,0:T(8,128)S(1)} %fusion.75), channel_id=1, replica_groups=mesh['seq'=64,'tensor'=4] {'tensor'}, use_global_device_ids=true, to_apply=%region_4.5 | all-reduce | flops 65536 | bytes 393216 | tf_op jit(solution)/shard_map/psum | solution.py:126
  127.7 51.0 %all-gather.5.cloned.1.call-done = bf16[64,64,512]{2,1,0:T(8,128)(2,1)} async-done(((bf16[1,64,512]{2,1,0:T(8,128)(2,1)}), bf16[64,64,512]{2,1,0:T(8,128)(2,1)}) %all-gather.5.cloned.1.call-update) | async-done | bytes 4194320 | tf_op jit(solution)/shard_map/all_gather | solution.py:120
  178.8 3.0 convolution_convert_fusion
  183.3 2.3 multiply_reduce_fusion.1
  187.5 3.1 fusion.5
  190.6 4.4 %fusion = (f32[2,512]{1,0:T(2,128)S(1)}, f32[1536,512,2]{1,0,2:T(8,128)S(1)}) fusion(f32[2,512]{1,0:T(2,128)S(1)} %get-tuple-element.20, f32[1536,512,2]{1,0,2:T(8,128)S(1)} %get-tuple-element.21, pred[512,1536]{0,1:T(8,128)(4,1)S(1)} %copy-done.5, bf16[64,2,8,256]{3,2,1,0:T(8,128)(2,1)S(1)} %bitcast.152, bf16[512,1,256]{2,0,1:T(8,128)(2,1)} %fusion.34, ...), kind=kOutput, calls=%fused_computation.4 | convolution fusion | flops 815528960 | bytes 14688256 | tf_op jit(solution)/shard_map/tngd,knd->ngtk/dot_general | solution.py:77
  195.0 3.8 %fusion.26 = f32[512,2,256]{2,0,1:T(8,128)S(1)} fusion(f32[1536,512,2]{1,0,2:T(8,128)S(1)} %get-tuple-element.23, f32[2,512]{1,0:T(2,128)S(1)} %get-tuple-element.22, f32[2,512]{1,0:T(2,128)S(1)} %get-tuple-element.20, f32[1536,512,2]{1,0,2:T(8,128)S(1)} %get-tuple-element.21, pred[512,1536]{0,1:T(8,128)(4,1)S(1)} %copy-done.5, ...), kind=kOutput, calls=%fused_computation.33 | convolution fusion | flops 819462144 | bytes 15212544 | tf_op jit(solution)/shard_map/ngtk,knd->tngd/dot_general | solution.py:80
  200.6 4.5 %fusion.76 = f32[64,64,512]{2,1,0:T(8,128)} fusion(bf16[64,16,64]{2,1,0:T(8,128)(2,1)S(1)} %bitcast.142, bf16[64,16,512]{2,1,0:T(8,128)(2,1)S(1)} %bitcast.141), kind=kOutput, calls=%fused_computation.116 | convolution fusion | flops 67108864 | bytes 9568256 | tf_op jit(solution)/shard_map/acr,ace->are/dot_general | solution.py:189
  205.1 5.2 %fusion.31 = bf16[256,2,512]{2,0,1:T(8,128)(2,1)S(1)} fusion(f32[2,512]{1,0:T(2,128)S(1)} %get-tuple-element.20, f32[1536,512,2]{1,0,2:T(8,128)} %copy-done.12, pred[512,1536]{0,1:T(8,128)(4,1)S(1)} %copy-done.5, bf16[512,1,256]{2,0,1:T(8,128)(2,1)} %fusion.34, bf16[512,1,256]{2,0,1:T(8,128)(2,1)} %collective-permute-done.4, ...), kind=kOutput, calls=%fused_computation.37 | convolution fusion | flops 814219264 | bytes 8392704 | tf_op jit(solution)/shard_map/ngtk,knd->tngd/dot_general | solution.py:76
  210.3 1.0 copy.52
  211.3 143.4 %reduce-scatter.2.cloned.1.call-done = f32[1,64,512]{2,1,0:T(8,128)} async-done(((f32[64,64,512]{2,1,0:T(8,128)}), f32[1,64,512]{2,1,0:T(8,128)}) %reduce-scatter.2.cloned.1.call-update) | async-done | bytes 131088 | tf_op jit(solution)/shard_map/reduce_scatter | solution.py:188
  (72 shorter events, 11.6 us)
Async XLA Ops:
  7.2 67.6 %copy-start = (bf16[3840,256]{1,0:T(8,128)(2,1)S(1)}, bf16[3840,256]{1,0:T(8,128)(2,1)}, u32[]{:S(2)}) copy-start(bf16[3840,256]{1,0:T(8,128)(2,1)} %param.13) | copy-start | bytes 5898244
  7.2 93.5 %all-gather.3.cloned.1.call-start = ((), (), s32[]{:S(2)}) async-start(), calls=%async_computation.1 | async-start | bytes 8519680 | tf_op jit(solution)/shard_map/all_gather | solution.py:119
  7.9 170.9 %all-gather.5.cloned.1.call-start = ((), (), s32[]{:S(2)}) async-start(), calls=%async_computation.2 | async-start | bytes 4259840 | tf_op jit(solution)/shard_map/all_gather | solution.py:120
  8.7 346.0 %reduce-scatter.2.cloned.1.call-start = ((), (), s32[]{:S(2)}) async-start(), calls=%async_computation.3 | async-start | bytes 8519680 | tf_op jit(solution)/shard_map/reduce_scatter | solution.py:188
  8.7 37.3 %collective-permute-start.6 = (s32[512]{0:T(512)}, s32[512]{0:T(512)S(1)}, u32[]{:S(2)}, u32[]{:S(2)}) collective-permute-start(s32[512]{0:T(512)} %param.20), channel_id=1, source_target_pairs={{0,4},{4,8},{8,12},{12,16},{16,20},{20,24},{24,28},{28,32},{32,36}... | collective-permute-start | bytes 6152 | tf_op jit(solution)/shard_map/ppermute | solution.py:39
  10.5 35.5 %collective-permute-start.5 = (s32[512]{0:T(512)}, s32[512]{0:T(512)S(1)}, u32[]{:S(2)}, u32[]{:S(2)}) collective-permute-start(s32[512]{0:T(512)} %param.20), channel_id=1, source_target_pairs={{0,8},{4,12},{8,16},{12,20},{16,24},{20,28},{24,32},{28,36},{32,40... | collective-permute-start | bytes 6152 | tf_op jit(solution)/shard_map/ppermute | solution.py:39
  14.5 34.0 %collective-permute-start.2 = (bf16[512,960]{0,1:T(8,128)(2,1)}, bf16[512,960]{0,1:T(8,128)(2,1)}, u32[]{:S(2)}, u32[]{:S(2)}) collective-permute-start(bf16[512,960]{0,1:T(8,128)(2,1)} %param.11), channel_id=1, source_target_pairs={{1,0},{2,1},{3,2},{0,3},{5,4},{6,5},{7,6},{4,7},{9,8},{10,9},{11,1... | collective-permute-start | bytes 2949128 | tf_op jit(solution)/shard_map/ppermute | solution.py:29
  15.1 24.9 %collective-permute-start = (bf16[512,960]{0,1:T(8,128)(2,1)}, bf16[512,960]{0,1:T(8,128)(2,1)}, u32[]{:S(2)}, u32[]{:S(2)}) collective-permute-start(bf16[512,960]{0,1:T(8,128)(2,1)} %param.11), channel_id=1, source_target_pairs={{0,1},{1,2},{2,3},{3,0},{4,5},{5,6},{6,7},{7,4},{8,9},{9,10},{10,1... | collective-permute-start | bytes 2949128 | tf_op jit(solution)/shard_map/ppermute | solution.py:27
  24.1 21.9 %copy-start.7 = (s32[512]{0:T(512)S(1)}, s32[512]{0:T(512)}, u32[]{:S(2)}) copy-start(s32[512]{0:T(512)} %param.20) | copy-start | bytes 6148
  24.1 42.3 %copy-start.4 = (bf16[512,960]{0,1:T(8,128)(2,1)S(1)}, bf16[512,960]{0,1:T(8,128)(2,1)}, u32[]{:S(2)}) copy-start(bf16[512,960]{0,1:T(8,128)(2,1)} %param.11) | copy-start | bytes 2949124
  40.0 26.3 %collective-permute-start.1 = (bf16[512,960]{0,1:T(8,128)(2,1)}, bf16[512,960]{0,1:T(8,128)(2,1)}, u32[]{:S(2)}, u32[]{:S(2)}) collective-permute-start(bf16[512,960]{0,1:T(8,128)(2,1)} %collective-permute-done), channel_id=1, source_target_pairs={{0,1},{1,2},{2,3},{3,0},{4,5},{5,6},{6,7},{7,4},{8,9},{9,10},{10,1... | collective-permute-start | bytes 2949128 | tf_op jit(solution)/shard_map/ppermute | solution.py:27
  74.8 3.6 copy-start.8
  74.8 11.7 %copy-start.2 = (bf16[4,512,960]{1,2,0:T(8,128)(2,1)S(1)}, bf16[4,512,960]{1,2,0:T(8,128)(2,1)}, u32[]{:S(2)}) copy-start(bf16[4,512,960]{1,2,0:T(8,128)(2,1)} %gather_fusion) | copy-start | bytes 11796484
  74.8 11.7 %copy-start.10 = (bf16[3840,256]{1,0:T(8,128)(2,1)S(1)}, bf16[3840,256]{1,0:T(8,128)(2,1)}, u32[]{:S(2)}) copy-start(bf16[3840,256]{1,0:T(8,128)(2,1)} %param.14) | copy-start | bytes 5898244
  80.4 107.0 %collective-permute-start.8 = (bf16[512,1,256]{0,2,1:T(8,128)(2,1)}, bf16[512,1,256]{0,2,1:T(8,128)(2,1)}, u32[]{:S(2)}, u32[]{:S(2)}) collective-permute-start(bf16[512,1,256]{0,2,1:T(8,128)(2,1)} %pad_maximum_fusion.1), channel_id=1, source_target_pairs={{0,4},{4,8},{8,12},{12,16},{16,20},{20,24},{24,28},{28,32},{32,36}... | collective-permute-start | bytes 786440 | tf_op jit(solution)/shard_map/ppermute | solution.py:39
  83.0 104.4 %collective-permute-start.7 = (bf16[512,1,256]{0,2,1:T(8,128)(2,1)}, bf16[512,1,256]{0,2,1:T(8,128)(2,1)}, u32[]{:S(2)}, u32[]{:S(2)}) collective-permute-start(bf16[512,1,256]{0,2,1:T(8,128)(2,1)} %pad_maximum_fusion.1), channel_id=1, source_target_pairs={{0,8},{4,12},{8,16},{12,20},{16,24},{20,28},{24,32},{28,36},{32,40... | collective-permute-start | bytes 786440 | tf_op jit(solution)/shard_map/ppermute | solution.py:39
  88.4 102.1 %collective-permute-start.4 = (bf16[512,1,256]{2,0,1:T(8,128)(2,1)}, bf16[512,1,256]{2,0,1:T(8,128)(2,1)}, u32[]{:S(2)}, u32[]{:S(2)}) collective-permute-start(bf16[512,1,256]{2,0,1:T(8,128)(2,1)} %fusion.34), channel_id=1, source_target_pairs={{0,4},{4,8},{8,12},{12,16},{16,20},{20,24},{24,28},{28,32},{32,36}... | collective-permute-start | bytes 786440 | tf_op jit(solution)/shard_map/ppermute | solution.py:39
  91.0 99.6 %collective-permute-start.3 = (bf16[512,1,256]{2,0,1:T(8,128)(2,1)}, bf16[512,1,256]{2,0,1:T(8,128)(2,1)}, u32[]{:S(2)}, u32[]{:S(2)}) collective-permute-start(bf16[512,1,256]{2,0,1:T(8,128)(2,1)} %fusion.34), channel_id=1, source_target_pairs={{0,8},{4,12},{8,16},{12,20},{16,24},{20,28},{24,32},{28,36},{32,40... | collective-permute-start | bytes 786440 | tf_op jit(solution)/shard_map/ppermute | solution.py:39
  178.8 3.8 %copy-start.3 = (bf16[4,512,960]{1,2,0:T(8,128)(2,1)S(1)}, bf16[4,512,960]{1,2,0:T(8,128)(2,1)}, u32[]{:S(2)}) copy-start(bf16[4,512,960]{1,2,0:T(8,128)(2,1)} %gather_fusion) | copy-start | bytes 11796484
  178.8 4.6 %copy-start.9 = (bf16[3840,512]{1,0:T(8,128)(2,1)S(1)}, bf16[3840,512]{1,0:T(8,128)(2,1)}, u32[]{:S(2)}) copy-start(bf16[3840,512]{1,0:T(8,128)(2,1)} %param.12) | copy-start | bytes 11796484
  185.6 1.4 copy-start.6
  186.0 1.5 copy-start.5
  187.4 3.1 copy-start.11
  190.5 4.5 %copy-start.12 = (f32[1536,512,2]{1,0,2:T(8,128)}, f32[1536,512,2]{1,0,2:T(8,128)S(1)}, u32[]{:S(2)}) copy-start(f32[1536,512,2]{1,0,2:T(8,128)S(1)} %get-tuple-element.21) | copy-start | bytes 18874372
  205.1 149.6 %copy-start.1 = (bf16[3840,256]{1,0:T(8,128)(2,1)S(1)}, bf16[3840,256]{1,0:T(8,128)(2,1)}, u32[]{:S(2)}) copy-start(bf16[3840,256]{1,0:T(8,128)(2,1)} %param.13) | copy-start | bytes 5898244
Sparse Core Ops, SparseCore 0:
  10.8 89.8 all-gather.2
  103.5 75.2 all-gather.4
  205.2 149.4 reduce-scatter.1
